TPU v7x, 128 devices: a whole 4x4x4 slice. The times are simulated.
128 devices in a mesh: sens: 8 (over z, core), layer: 16 (over y, x).
Axes of the slice: x: 4, y: 4, z: 4, core: 2. Of those that a mesh axis runs over, the one named last changes fastest.
Arguments:
- slopes: bfloat16 [1024, 63600], P('layer', 'sens'), may hold values from -7 to 7
- valid: int32 [63600], P('sens'), may hold values from 0 to 1
- sensor_map: int32 [63600], P('sens'), may hold values from 0 to 5, as said below
- reconstructor: bfloat16 [16000, 63600], P('layer', 'sens'), may hold values from -0.0234375 to 0.0234375
- fitting: bfloat16 [7800, 16000], P('sens', 'layer'), may hold values from -0.046875 to 0.046875
Outputs:
- commands: float32 [1024, 7800], P(('sens', 'layer'))
Inputs may be any that keep to these rules, and one draw needn't show every extreme that they name: `sensor_map`: both slopes of a subaperture (indices 2 i and 2 i + 1) belong to one sensor.
All inputs are finite; a program needn't handle non-finite values.
Results may differ from a plain program's by a relative error of at most 0.02.
Values may be sent and summed in bfloat16 or wider, within the bound.
No kernel may reach another device: no remote copies, remote signals or barrier semaphores. Data moves between devices by JAX's collectives and lax.ppermute only.
A program may use at most 192 MiB of HBM per device.

v0:
```python
import jax
import jax.numpy as jnp
from jax import lax
from jax.sharding import PartitionSpec as P

SENSORS = 6


def copy_for_each(x, axis):
    length = lax.axis_size(axis)
    return lax.all_to_all(jnp.broadcast_to(x[None], (length, *x.shape)), axis, 0, 0, tiled=True)


def taken_together(x, axis):
    everything = copy_for_each(x, axis)
    return jnp.sum(everything.astype(jnp.float32), axis=0)


def cut_along(x, dim, length):
    dims = x.shape
    blocks = x.reshape(*dims[:dim], length, dims[dim] // length, *dims[dim + 1 :])
    return jnp.moveaxis(blocks, dim, 0)


def summed_on_arrival(x, axis, dim):
    blocks = cut_along(x, dim, lax.axis_size(axis))
    arrived = lax.all_to_all(blocks, axis, split_axis=0, concat_axis=0, tiled=True)
    return arrived.astype(jnp.float32).sum(axis=0)


def contract(left, right):
    return lax.dot_general(
        left, right, (((1,), (1,)), ((), ())), preferred_element_type=jnp.float32
    )


def cleaned(block, live, onehot_full, sums, counts):
    means = sums / jnp.maximum(counts, 1.0)
    spread = lax.dot_general(
        means, onehot_full, (((1,), (1,)), ((), ())), precision=lax.Precision.HIGHEST
    )
    return (live.astype(jnp.float32)[None, :] * (block.astype(jnp.float32) - spread)).astype(
        jnp.bfloat16
    )


def per_device(slopes, valid, sensor_map, reconstructor, fitting):
    width_local = slopes.shape[1]
    start = lax.axis_index("sens") * width_local
    parity = (lax.iota(jnp.int32, width_local) + start) % 2
    group = sensor_map * 2 + parity
    labels = lax.iota(jnp.int32, 2 * SENSORS)
    onehot_full = (group[:, None] == labels[None, :]).astype(jnp.float32)
    onehot_low = onehot_full.astype(jnp.bfloat16)
    live = valid.astype(jnp.bfloat16)
    count_terms = jnp.dot(live[None, :], onehot_low, preferred_element_type=jnp.float32)[0]
    whole = lax.all_gather(slopes, "layer", axis=0, tiled=True)
    masked = whole * live[None, :]
    sums = jnp.dot(masked, onehot_low, preferred_element_type=jnp.float32)
    sums, counts = (
        taken_together(sums.astype(jnp.bfloat16), "sens").astype(jnp.float32),
        taken_together(count_terms.astype(jnp.bfloat16), "sens").astype(jnp.float32),
    )
    clean = cleaned(whole, live, onehot_full, sums, counts)
    partial_points = contract(clean, reconstructor)
    points = summed_on_arrival(partial_points.astype(jnp.bfloat16), "sens", 0).astype(jnp.bfloat16)
    partial_commands = contract(points, lax.all_gather(fitting, "sens", axis=0, tiled=True))
    return summed_on_arrival(partial_commands.astype(jnp.bfloat16), "layer", 0)


def solution(mesh):
    placed = (P("layer", "sens"), P("sens"), P("sens"), P("layer", "sens"), P("sens", "layer"))
    return jax.shard_map(
        per_device,
        mesh=mesh,
        in_specs=placed,
        out_specs=P(("sens", "layer"), None),
        check_vma=False,
    )
```

profile of v0, /device:TPU:0, one launch (start us, length us, event | category | flops | bytes accessed | tf_op | source)
XLA Modules:
  0.0 284.0 jit_solution(14590893099064575598)
XLA Ops:
  6.5 0.0 all-gather.4.cloned.1.call-start
  6.5 0.7 all-gather.4.cloned.1.call-update
  7.3 0.0 all-gather.6.cloned.1.call-start
  7.3 0.7 all-gather.6.cloned.1.call-update
  8.0 0.8 fusion.17
  8.8 0.2 fusion.6
  9.0 10.5 %all_to_all.21 = bf16[8,1,12]{2,1,0:T(2,128)(2,1)S(1)} all-to-all(bf16[8,1,12]{2,1,0:T(2,128)(2,1)S(1)} %broadcast_in_dim.5), channel_id=1, replica_groups=mesh['sens'=8,'layer'=16] {'sens'}, dimensions={0} | all-to-all | bytes 384 | tf_op jit(solution)/shard_map/all_to_all | solution.py:11
  19.5 102.3 %all-gather.4.cloned.1.call-done = bf16[1024,7950]{1,0:T(8,128)(2,1)} async-done(((bf16[64,7950]{1,0:T(8,128)(2,1)}), bf16[1024,7950]{1,0:T(8,128)(2,1)}) %all-gather.4.cloned.1.call-update) | async-done | bytes 16281616 | tf_op jit(solution)/shard_map/all_gather | solution.py:57
  121.9 10.0 %fusion.3 = bf16[1024,12]{0,1:T(8,128)(2,1)S(1)} fusion(bf16[1024,7950]{1,0:T(8,128)(2,1)} %all-gather.4.cloned.1.call-done, bf16[7950]{0:T(1024)(128)(2,1)S(1)} %get-tuple-element.6, s32[7950]{0:T(1024)S(1)} %get-tuple-element.7), kind=kOutput, calls=%fused_computation.8 | convolution fusion | flops 203818496 | bytes 16353876 | tf_op jit(solution)/shard_map/dot_general | solution.py:59
  131.9 0.8 broadcast_in_dim.4
  132.7 4.4 %all-to-all-start = ((bf16[8,1024,12]{1,2,0:T(8,128)(2,1)}), bf16[8,1024,12]{1,2,0:T(8,128)(2,1)S(1)}, u32[]{:S(2)}, u32[]{:S(2)}) async-start(bf16[8,1024,12]{1,2,0:T(8,128)(2,1)} %broadcast_in_dim.4), calls=%async_computation | async-start | bytes 524288 | tf_op jit(solution)/shard_map/all_to_all | solution.py:11
  137.1 22.4 %copy.24 = bf16[1024,7950]{0,1:T(8,128)(2,1)} copy(bf16[1024,7950]{1,0:T(8,128)(2,1)} %all-gather.4.cloned.1.call-done) | data formatting | bytes 32563200 | tf_op jit(solution)/shard_map/all_gather | solution.py:57
  159.5 0.0 all-to-all-done
  159.6 19.0 %multiply_convert_fusion = bf16[1024,7950]{0,1:T(8,128)(2,1)S(1)} fusion(bf16[1024,7950]{0,1:T(8,128)(2,1)} %copy.24, f32[7950]{0:T(1024)S(1)} %get-tuple-element.5, s32[7950]{0:T(1024)S(1)} %get-tuple-element.7, f32[1024,12]{0,1:T(8,128)S(1)} %convert_reduce_fusion.1, f32[12]{0:T(128)S(1)} %broadcast_maximum_fusion), kind=kOutput, calls=%fused_computation | convolution fusion | flops 1204946048 | bytes 32676000 | tf_op jit(solution)/shard_map/dot_general | solution.py:39
  178.5 20.7 %convert_bitcast_fusion = bf16[125,8,8,128]{3,2,1,0:T(8,128)(2,1)S(1)} fusion(bf16[1024,7950]{0,1:T(8,128)(2,1)S(1)} %multiply_convert_fusion, bf16[1000,7950]{1,0:T(8,128)(2,1)} %param.8), kind=kOutput, calls=%fused_computation.7 | convolution fusion | flops 16282624000 | bytes 34229600 | tf_op jit(solution)/shard_map/dot_general | solution.py:32
  199.3 1.6 copy.33
  200.9 4.7 %all-to-all-start.2 = ((bf16[8,128,1000]{1,2,0:T(8,128)(2,1)}), bf16[8,128,1000]{1,2,0:T(8,128)(2,1)S(1)}, u32[]{:S(2)}, u32[]{:S(2)}) async-start(bf16[8,128,1000]{1,2,0:T(8,128)(2,1)} %bitcast.16), calls=%async_computation.2 | async-start | bytes 4096000 | tf_op jit(solution)/shard_map/all_to_all | solution.py:27
  205.7 2.3 all-gather.6.cloned.1.call-done
  208.0 20.5 %reshape.30 = bf16[7800,1000]{1,0:T(8,128)(2,1)} reshape(bf16[8,975,1000]{2,1,0:T(8,128)(2,1)} %all-gather.6.cloned.1.call-done) | data formatting | bytes 31200000
  228.5 3.8 %all-to-all-done.2 = bf16[8,128,1000]{1,2,0:T(8,128)(2,1)S(1)} async-done(((bf16[8,128,1000]{1,2,0:T(8,128)(2,1)}), bf16[8,128,1000]{1,2,0:T(8,128)(2,1)S(1)}, u32[]{:S(2)}, u32[]{:S(2)}) %all-to-all-start.2) | async-done | bytes 2048032 | tf_op jit(solution)/shard_map/all_to_all | solution.py:27
  232.3 0.4 reduce_sum.41
  232.7 9.3 %convolution_convert_fusion = bf16[128,7800]{0,1:T(8,128)(2,1)} fusion(bf16[128,1000]{0,1:T(8,128)(2,1)S(1)} %reduce_sum.41, bf16[7800,1000]{1,0:T(8,128)(2,1)} %reshape.30), kind=kOutput, calls=%fused_computation.3 | convolution fusion | flops 1997798400 | bytes 17852800 | tf_op jit(solution)/shard_map/dot_general | solution.py:32
  242.0 2.9 %copy.28 = bf16[128,7800]{1,0:T(8,128)(2,1)S(1)} copy(bf16[128,7800]{0,1:T(8,128)(2,1)} %convolution_convert_fusion) | data formatting | bytes 3993600 | tf_op jit(solution)/shard_map/convert_element_type | solution.py:68
  244.9 31.2 %all_to_all.22 = bf16[16,8,7800]{2,1,0:T(8,128)(2,1)S(1)} all-to-all(bf16[16,8,7800]{2,1,0:T(8,128)(2,1)S(1)} %bitcast.17), channel_id=1, replica_groups=mesh['sens'=8,'layer'=16] {'layer'}, dimensions={0} | all-to-all | bytes 3993600 | tf_op jit(solution)/shard_map/all_to_all | solution.py:27
  276.2 1.0 convert_reduce_fusion
  (5 shorter events, 0.1 us)
Async XLA Ops:
  6.5 115.3 %all-gather.4.cloned.1.call-start = ((), (), s32[]{:S(2)}) async-start(), calls=%async_computation.4 | async-start | bytes 17547264 | tf_op jit(solution)/shard_map/all_gather | solution.py:57
  7.3 200.7 %all-gather.6.cloned.1.call-start = ((), (), s32[]{:S(2)}) async-start(), calls=%async_computation.5 | async-start | bytes 17989632 | tf_op jit(solution)/shard_map/all_gather | solution.py:67
  132.7 26.8 %all-to-all-start = ((bf16[8,1024,12]{1,2,0:T(8,128)(2,1)}), bf16[8,1024,12]{1,2,0:T(8,128)(2,1)S(1)}, u32[]{:S(2)}, u32[]{:S(2)}) async-start(bf16[8,1024,12]{1,2,0:T(8,128)(2,1)} %broadcast_in_dim.4), calls=%async_computation | async-start | bytes 524288 | tf_op jit(solution)/shard_map/all_to_all | solution.py:11
  200.9 31.4 %all-to-all-start.2 = ((bf16[8,128,1000]{1,2,0:T(8,128)(2,1)}), bf16[8,128,1000]{1,2,0:T(8,128)(2,1)S(1)}, u32[]{:S(2)}, u32[]{:S(2)}) async-start(bf16[8,128,1000]{1,2,0:T(8,128)(2,1)} %bitcast.16), calls=%async_computation.2 | async-start | bytes 4096000 | tf_op jit(solution)/shard_map/all_to_all | solution.py:27
Sparse Core Ops, SparseCore 0:
  9.5 112.3 all-gather.3
  123.5 84.3 all-gather.5
where the time goes:
time: 285 us; the launch traced here: 284 us
  waiting for transfers between devices  110 us (39%)
  matrix products  59.2 us (21%)
  local copies, waits for them, and re-layouts  48.3 us (17%)
  blocking collectives  41.7 us (15%)
  between operations  13.5 us (5%)
  starting transfers between devices  9.2 us (3%)
    all_gather x1, waiting for transfers between devices, per_device(): whole = lax.all_gather(slopes, 'layer', axis=0, tiled=True)  102 us
    all_to_all x1, blocking collectives, summed_on_arrival(): lax.all_to_all(blocks, axis, split_axis=0, concat_axis=0, tiled=True)  31.2 us
    dot_general x2, matrix products, contract(): lax.dot_general(left, right, (((1,), (1,)), ((), ())), preferred_element_...  30 us
    all_gather x1, local copies, waits for them, and re-layouts, per_device(): whole = lax.all_gather(slopes, 'layer', axis=0, tiled=True)  22.4 us
    unnamed x1, local copies, waits for them, and re-layouts  20.5 us
    dot_general x1, matrix products, cleaned(): lax.dot_general(means, onehot_full, (((1,), (1,)), ((), ())), precision=l...  19 us
    all_to_all x1, blocking collectives, copy_for_each(): lax.all_to_all(jnp.broadcast_to(x[None], (length, *x.shape)), axis, 0, 0,...  10.5 us
    dot_general x1, matrix products, per_device(): sums = jnp.dot(masked, onehot_low, preferred_element_type=jnp.float32)  10 us
  transfers between devices with their start and end apart: 4, of which 3 were waited for; matrix products, arithmetic and copies ran while one was open for 34% of the time, Pallas kernels for 0%

commit v1 on v0

--- a/solution.py
+++ b/solution.py
@@ -54,7 +54,9 @@
     onehot_low = onehot_full.astype(jnp.bfloat16)
     live = valid.astype(jnp.bfloat16)
     count_terms = jnp.dot(live[None, :], onehot_low, preferred_element_type=jnp.float32)[0]
-    whole = lax.all_gather(slopes, "layer", axis=0, tiled=True)
+    whole = jnp.concatenate(
+        lax.all_to_all(jnp.stack([slopes] * lax.axis_size("layer")), "layer", 0, 0), axis=0
+    )
     masked = whole * live[None, :]
     sums = jnp.dot(masked, onehot_low, preferred_element_type=jnp.float32)
     sums, counts = (

time: 285 us -> 461 us (1.62)
  waiting for transfers between devices: 110 us -> 247 us
  blocking collectives: 41.7 us -> 71.7 us
  local copies, waits for them, and re-layouts: 48.3 us -> 55.7 us
    all_to_all x1, waiting for transfers between devices: 3.81 us -> 246 us  [per_device(): lax.all_to_all(jnp.stack([slopes] * lax.axis_size('layer')), 'layer', 0, 0)]
    all_gather x1 -> x0, waiting for transfers between devices: 102 us -> none  [per_device(): whole = lax.all_gather(slopes, 'layer', axis=0, tiled=True)]
    all_to_all x1 -> x2, blocking collectives: 31.2 us -> 61.3 us  [summed_on_arrival(): lax.all_to_all(blocks, axis, split_axis=0, concat_axis=0, tiled=True)]
    all_gather x1 -> x0, local copies, waits for them, and re-layouts: 22.4 us -> none  [per_device(): whole = lax.all_gather(slopes, 'layer', axis=0, tiled=True)]
    reshape x0 -> x1, local copies, waits for them, and re-layouts: none -> 22.2 us  [per_device(): jnp.concatenate(lax.all_to_all(jnp.stack([slopes] * lax.axis_size('layer'...]
    another operation x0 -> x1, local copies, waits for them, and re-layouts: none -> 8.79 us  [per_device(): jnp.stack([slopes] * lax.axis_size('layer'))]
  transfers between devices with their start and end apart: 4 -> 3, of which waited for: 3 -> 1; matrix products, arithmetic and copies ran while one was open for 34% -> 18% of each run, Pallas kernels for 0% -> 0%
where the time goes in v1:
time: 461 us; the launch traced here: 460 us
  waiting for transfers between devices  247 us (54%)
  blocking collectives  71.7 us (16%)
  matrix products  58.9 us (13%)
  local copies, waits for them, and re-layouts  55.7 us (12%)
  between operations  13.5 us (3%)
  starting transfers between devices  10.6 us (2%)
    all_to_all x1, waiting for transfers between devices, per_device(): lax.all_to_all(jnp.stack([slopes] * lax.axis_size('layer')), 'layer', 0, 0)  246 us
    all_to_all x2, blocking collectives, summed_on_arrival(): lax.all_to_all(blocks, axis, split_axis=0, concat_axis=0, tiled=True)  61.3 us
    dot_general x2, matrix products, contract(): lax.dot_general(left, right, (((1,), (1,)), ((), ())), preferred_element_...  29.8 us
    reshape x1, local copies, waits for them, and re-layouts, per_device(): jnp.concatenate(lax.all_to_all(jnp.stack([slopes] * lax.axis_size('layer'...  22.2 us
    unnamed x1, local copies, waits for them, and re-layouts  20.6 us
    dot_general x1, matrix products, cleaned(): lax.dot_general(means, onehot_full, (((1,), (1,)), ((), ())), precision=l...  18.9 us
    all_to_all x1, blocking collectives, copy_for_each(): lax.all_to_all(jnp.broadcast_to(x[None], (length, *x.shape)), axis, 0, 0,...  10.5 us
    dot_general x1, matrix products, per_device(): sums = jnp.dot(masked, onehot_low, preferred_element_type=jnp.float32)  10 us
  transfers between devices with their start and end apart: 3, of which 1 were waited for; matrix products, arithmetic and copies ran while one was open for 18% of the time, Pallas kernels for 0%

profile of v1, /device:TPU:0, one launch (start us, length us, event | category | flops | bytes accessed | tf_op | source)
XLA Modules:
  0.0 459.7 jit_solution(1127645338708991922)
XLA Ops:
  6.5 0.0 all-gather.3.cloned.1.call-start
  6.5 0.7 all-gather.3.cloned.1.call-update
  7.3 0.8 fusion.17
  8.1 0.2 fusion.6
  8.3 10.5 %all_to_all.26 = bf16[8,1,12]{2,1,0:T(2,128)(2,1)S(1)} all-to-all(bf16[8,1,12]{2,1,0:T(2,128)(2,1)S(1)} %broadcast_in_dim.5), channel_id=1, replica_groups=mesh['sens'=8,'layer'=16] {'sens'}, dimensions={0} | all-to-all | bytes 384 | tf_op jit(solution)/shard_map/all_to_all | solution.py:11
  18.8 8.8 %stack.2 = bf16[16,64,7950]{2,1,0:T(8,128)(2,1)} broadcast(bf16[64,7950]{1,0:T(8,128)(2,1)} %param.5), dimensions={1,2} | broadcast | bytes 17299200 | tf_op jit(solution)/shard_map/stack | solution.py:58
  27.6 7.0 %all-to-all-start = ((bf16[16,64,7950]{2,1,0:T(8,128)(2,1)}), bf16[16,64,7950]{2,1,0:T(8,128)(2,1)}, u32[]{:S(2)}, u32[]{:S(2)}) async-start(bf16[16,64,7950]{2,1,0:T(8,128)(2,1)} %stack.2), calls=%async_computation | async-start | bytes 33030144 | tf_op jit(solution)/shard_map/all_to_all | solution.py:58
  34.6 246.4 %all-to-all-done = bf16[16,64,7950]{2,1,0:T(8,128)(2,1)} async-done(((bf16[16,64,7950]{2,1,0:T(8,128)(2,1)}), bf16[16,64,7950]{2,1,0:T(8,128)(2,1)}, u32[]{:S(2)}, u32[]{:S(2)}) %all-to-all-start) | async-done | bytes 16281632 | tf_op jit(solution)/shard_map/all_to_all | solution.py:58
  281.0 10.0 %fusion.3 = bf16[1024,12]{0,1:T(8,128)(2,1)S(1)} fusion(bf16[1024,7950]{1,0:T(8,128)(2,1)} %bitcast, bf16[7950]{0:T(1024)(128)(2,1)S(1)} %get-tuple-element.6, s32[7950]{0:T(1024)S(1)} %get-tuple-element.7), kind=kOutput, calls=%fused_computation.8 | convolution fusion | flops 203818496 | bytes 16353876 | tf_op jit(solution)/shard_map/dot_general | solution.py:61
  291.0 0.8 broadcast_in_dim.4
  291.8 3.6 all-to-all-start.1
  295.4 22.2 %copy.28 = bf16[1024,7950]{0,1:T(8,128)(2,1)} copy(bf16[1024,7950]{1,0:T(8,128)(2,1)} %bitcast) | data formatting | bytes 32563200 | tf_op jit(solution)/shard_map/reshape | solution.py:57
  317.6 0.0 all-to-all-done.1
  317.7 18.9 %multiply_convert_fusion = bf16[1024,7950]{0,1:T(8,128)(2,1)S(1)} fusion(bf16[1024,7950]{0,1:T(8,128)(2,1)} %copy.28, f32[7950]{0:T(1024)S(1)} %get-tuple-element.5, s32[7950]{0:T(1024)S(1)} %get-tuple-element.7, f32[1024,12]{0,1:T(8,128)S(1)} %convert_reduce_fusion.1, f32[12]{0:T(128)S(1)} %broadcast_maximum_fusion), kind=kOutput, calls=%fused_computation | convolution fusion | flops 1204946048 | bytes 32676000 | tf_op jit(solution)/shard_map/dot_general | solution.py:39
  336.6 20.5 %convert_bitcast_fusion = bf16[125,8,8,128]{3,2,1,0:T(8,128)(2,1)S(1)} fusion(bf16[1024,7950]{0,1:T(8,128)(2,1)S(1)} %multiply_convert_fusion, bf16[1000,7950]{1,0:T(8,128)(2,1)} %param.8), kind=kOutput, calls=%fused_computation.7 | convolution fusion | flops 16282624000 | bytes 34229600 | tf_op jit(solution)/shard_map/dot_general | solution.py:32
  357.1 0.4 copy.37
  357.4 31.3 %all_to_all.27 = bf16[8,128,1000]{1,2,0:T(8,128)(2,1)S(1)} all-to-all(bf16[8,128,1000]{1,2,0:T(8,128)(2,1)S(1)} %bitcast.17), channel_id=1, replica_groups=mesh['sens'=8,'layer'=16] {'sens'}, dimensions={0} | all-to-all | bytes 4096000 | tf_op jit(solution)/shard_map/all_to_all | solution.py:27
  388.8 0.4 reduce_sum.41
  389.2 0.0 all-gather.3.cloned.1.call-done
  389.2 20.6 %reshape.36 = bf16[7800,1000]{1,0:T(8,128)(2,1)} reshape(bf16[8,975,1000]{2,1,0:T(8,128)(2,1)} %all-gather.3.cloned.1.call-done) | data formatting | bytes 31200000
  409.8 9.3 %convolution_convert_fusion = bf16[128,7800]{0,1:T(8,128)(2,1)} fusion(bf16[128,1000]{0,1:T(8,128)(2,1)S(1)} %reduce_sum.41, bf16[7800,1000]{1,0:T(8,128)(2,1)} %reshape.36), kind=kOutput, calls=%fused_computation.3 | convolution fusion | flops 1997798400 | bytes 17852800 | tf_op jit(solution)/shard_map/dot_general | solution.py:32
  419.1 2.9 copy.32
  422.0 29.9 %all_to_all.28 = bf16[16,8,7800]{2,1,0:T(8,128)(2,1)S(1)} all-to-all(bf16[16,8,7800]{2,1,0:T(8,128)(2,1)S(1)} %bitcast.18), channel_id=1, replica_groups=mesh['sens'=8,'layer'=16] {'layer'}, dimensions={0} | all-to-all | bytes 3993600 | tf_op jit(solution)/shard_map/all_to_all | solution.py:27
  451.9 1.0 convert_reduce_fusion
  (5 shorter events, 0.1 us)
Async XLA Ops:
  6.5 382.6 %all-gather.3.cloned.1.call-start = ((), (), s32[]{:S(2)}) async-start(), calls=%async_computation.5 | async-start | bytes 17989632 | tf_op jit(solution)/shard_map/all_gather | solution.py:69
  27.6 253.4 %all-to-all-start = ((bf16[16,64,7950]{2,1,0:T(8,128)(2,1)}), bf16[16,64,7950]{2,1,0:T(8,128)(2,1)}, u32[]{:S(2)}, u32[]{:S(2)}) async-start(bf16[16,64,7950]{2,1,0:T(8,128)(2,1)} %stack.2), calls=%async_computation | async-start | bytes 33030144 | tf_op jit(solution)/shard_map/all_to_all | solution.py:58
  291.8 25.8 %all-to-all-start.1 = ((bf16[8,1024,12]{1,2,0:T(8,128)(2,1)}), bf16[8,1024,12]{1,2,0:T(8,128)(2,1)S(1)}, u32[]{:S(2)}, u32[]{:S(2)}) async-start(bf16[8,1024,12]{1,2,0:T(8,128)(2,1)} %broadcast_in_dim.4), calls=%async_computation.1 | async-start | bytes 524288 | tf_op jit(solution)/shard_map/all_to_all | solution.py:11
Sparse Core Ops, SparseCore 0:
  9.0 84.3 all-gather.2
